TPU v7x, 32 devices: a whole 2x2x4 slice. The times are simulated.
32 devices in a mesh: group: 4 (over y, core), blk: 8 (over z, x).
Axes of the slice: x: 2, y: 2, z: 4, core: 2. Of those that a mesh axis runs over, the one named last changes fastest.
Arguments:
- features: bfloat16 [1024, 2048], P('blk', 'group'), may hold values from -6 to 6
- weight: bfloat16 [2048, 256], P('group'), may hold values from -0.125 to 0.125
- queue: bfloat16 [16384, 256], P(('group', 'blk')), may hold values from -0.5 to 0.5, as said below
- fresh_keys: bfloat16 [1024, 256], P('blk'), may hold values from -0.3984375 to 0.3984375
- positives: int32 [1024], P('blk'), may hold values from 0 to 1023, each once
- write_slot: int32 [1], replicated, may hold values from 0 to 15360
Outputs:
- query_loss: float32 [1024], P('blk')
- weight_grad: float32 [2048, 256], P(('group', 'blk'))
- new_queue: bfloat16 [16384, 256], P(('group', 'blk'))
Inputs may be any that keep to these rules, and one draw needn't show every extreme that they name: `queue`: scaled item keys.
All inputs are finite; a program needn't handle non-finite values.
Results may differ from a plain program's by a relative error of at most 0.003.
The roundings to bfloat16 on the way count: a program that leaves them out, or rounds other values in their place, can miss the bound.
Values may be sent and summed in bfloat16 or wider, within the bound.
No kernel may reach another device: no remote copies, remote signals or barrier semaphores. Data moves between devices by JAX's collectives and lax.ppermute only.
A program may use at most 64 MiB of HBM per device.

v0:
```python
import jax
import jax.numpy as jnp
from jax import lax
from jax.sharding import PartitionSpec as P

epsilon = 1e-06
inverse_sharpness_factor = 8.0


def local(features, weight, queue, fresh_keys, positives, write_slot):
    partial_proj = jnp.dot(features, weight, preferred_element_type=jnp.float32)
    projected = lax.psum(partial_proj, "group")
    length = jnp.sqrt(jnp.sum(projected * projected, axis=1, keepdims=True) + epsilon)
    unit_rows = projected / length
    query_rows = unit_rows.astype(jnp.bfloat16)
    all_fresh = lax.all_gather(fresh_keys, "blk", axis=0, tiled=True)
    all_queries = lax.all_gather(query_rows, "blk", axis=0, tiled=True)
    query_total = all_queries.shape[0]
    key_width = all_queries.shape[1]
    blk_count = lax.axis_size("blk")
    block_rows = 512
    query_blocks = all_queries.reshape(query_total // block_rows, block_rows, key_width)

    def score_block(carry, rows_now):
        similarity_matrix = jnp.einsum(
            "qc,sc->qs", rows_now, queue, preferred_element_type=jnp.float32
        )
        exponentials = jnp.exp(inverse_sharpness_factor * similarity_matrix)
        denominator = jnp.sum(exponentials, axis=1)
        numerator = jnp.dot(
            exponentials.astype(jnp.bfloat16), queue, preferred_element_type=jnp.float32
        )
        return (carry, (numerator, denominator))

    _, (numer_blocks, denom_blocks) = lax.scan(score_block, jnp.float32(0.0), query_blocks)
    numer_all = numer_blocks.reshape(query_total, key_width)
    denom_all = denom_blocks.reshape(query_total)
    numer_part, denom_part = (
        lax.psum_scatter(numer_all, "blk", scatter_dimension=0, tiled=True),
        lax.psum_scatter(denom_all, "blk", scatter_dimension=0, tiled=True),
    )
    numerator, denominator = lax.psum((numer_part, denom_part), "group")
    paired_encodings = jnp.take(all_fresh, positives, axis=0).astype(jnp.float32)
    pair_score = inverse_sharpness_factor * jnp.sum(
        query_rows.astype(jnp.float32) * paired_encodings, axis=1
    )
    pair_weight = jnp.exp(pair_score)
    probability_mass = pair_weight + denominator
    query_loss = jnp.log(probability_mass) - pair_score
    query_derivative = inverse_sharpness_factor * (
        (pair_weight[:, None] * paired_encodings + numerator) / probability_mass[:, None]
        - paired_encodings
    )
    along = jnp.sum(query_derivative * unit_rows, axis=1, keepdims=True)
    grad_projected = ((query_derivative - along * unit_rows) / length).astype(jnp.bfloat16)
    weight_grad = lax.psum_scatter(
        lax.dot_general(
            features, grad_projected, (((0,), (0,)), ((), ())), preferred_element_type=jnp.float32
        ),
        "blk",
        scatter_dimension=0,
        tiled=True,
    )
    slot_count = queue.shape[0]
    device_index = lax.axis_index("group") * blk_count + lax.axis_index("blk")
    window_start = write_slot[0]
    slot_index = device_index * slot_count + jnp.arange(slot_count, dtype=jnp.int32)
    offset = slot_index - window_start
    in_window = (offset >= 0) & (offset < query_total)
    picked = jnp.take(all_fresh, jnp.clip(offset, 0, query_total - 1), axis=0)
    new_queue = jnp.where(in_window[:, None], picked, queue)
    return (query_loss, weight_grad, new_queue)


def solution(mesh):
    in_specs = (
        P("blk", "group"),
        P("group", None),
        P(("group", "blk"), None),
        P("blk", None),
        P("blk"),
        P(),
    )
    out_specs = (P("blk"), P(("group", "blk"), None), P(("group", "blk"), None))
    return jax.shard_map(local, mesh=mesh, in_specs=in_specs, out_specs=out_specs, check_vma=False)
```

profile of v0, /device:TPU:0, one launch (start us, length us, event | category | flops | bytes accessed | tf_op | source)
XLA Modules:
  0.0 252.1 jit_solution(920039892036683181)
XLA Ops:
  7.2 0.0 copy-start
  7.2 0.0 all-reduce.4.cloned.1.call-start
  7.2 0.9 copy-done
  8.1 1.7 fusion.20
  9.9 0.0 copy-start.7
  9.9 0.0 copy-start.6
  9.9 0.0 all-reduce.4.cloned.1.call-update
  9.9 0.0 reduce-scatter.5.cloned.1.call-start
  9.9 0.6 copy-done.7
  10.6 0.2 copy-done.6
  10.7 33.0 %all_gather.6 = bf16[1024,256]{1,0:T(8,128)(2,1)S(1)} all-gather(bf16[128,256]{1,0:T(8,128)(2,1)S(1)} %copy-done.6), channel_id=1, replica_groups=mesh['group'=4,'blk'=8] {'blk'}, dimensions={0}, use_global_device_ids=true | all-gather | bytes 589824 | tf_op jit(solution)/shard_map/all_gather | solution.py:16
  43.8 0.8 gather_fusion
  44.6 0.8 all-reduce.4.cloned.1.call-done
  45.4 1.1 multiply_reduce_fusion.1
  46.5 0.0 copy-done.2
  46.5 0.2 fusion.6
  46.7 0.0 copy-start.1
  46.7 31.5 %all_gather.7 = bf16[1024,256]{1,0:T(8,128)(2,1)S(1)} all-gather(bf16[128,256]{1,0:T(8,128)(2,1)S(1)} %get-tuple-element.53), channel_id=1, replica_groups=mesh['group'=4,'blk'=8] {'blk'}, dimensions={0}, use_global_device_ids=true | all-gather | bytes 589824 | tf_op jit(solution)/shard_map/all_gather | solution.py:17
  78.2 0.0 copy-done.1
  78.2 1.6 while.12
  78.3 0.4 fusion.35
  78.7 0.3 fusion.36
  79.0 0.4 fusion.35
  79.5 0.3 fusion.36
  79.8 0.0 copy-start.3
  79.8 1.0 copy-done.3
  80.8 0.0 reduce-scatter.5.cloned.1.call-update
  80.8 0.0 all-reduce.6.cloned.1.call-start
  80.9 0.0 copy-start.8
  80.9 0.6 copy-done.8
  81.6 0.6 dynamic-slice
  82.8 21.5 %all-reduce = f32[1024]{0:T(1024)S(1)} all-reduce(f32[1024]{0:T(1024)S(1)} %bitcast.43), channel_id=2, replica_groups=mesh['group'=4,'blk'=8] {'blk'}, use_global_device_ids=true, to_apply=%region_6.7.clone | all-reduce | flops 1024 | bytes 8192
  104.3 0.1 dynamic-slice.1
  104.4 6.0 %psum.22 = f32[128]{0:T(128)S(1)} all-reduce(f32[128]{0:T(128)S(1)} %dynamic-slice.1), channel_id=1, replica_groups=mesh['group'=4,'blk'=8] {'group'}, use_global_device_ids=true, to_apply=%region_7.8 | all-reduce | flops 128 | bytes 1024 | tf_op jit(solution)/shard_map/psum | solution.py:42
  110.4 35.3 %reduce-scatter.5.cloned.1.call-done = f32[128,256]{1,0:T(8,128)} async-done(((f32[1024,256]{1,0:T(8,128)}), f32[128,256]{1,0:T(8,128)}) %reduce-scatter.5.cloned.1.call-update) | async-done | bytes 131088 | tf_op jit(solution)/shard_map/reduce_scatter | solution.py:39
  145.7 0.0 all-reduce.6.cloned.1.call-update
  145.7 0.0 reduce-scatter.7.cloned.1.call-start
  145.7 0.5 fusion.15
  146.3 32.4 %all-reduce.6.cloned.1.call-done = f32[128,256]{1,0:T(8,128)} async-done(((f32[128,256]{1,0:T(8,128)}), f32[128,256]{1,0:T(8,128)}) %all-reduce.6.cloned.1.call-update) | async-done | bytes 131088 | tf_op jit(solution)/shard_map/psum | solution.py:42
  178.7 1.2 multiply_reduce_fusion
  179.9 0.0 copy-done.4
  179.9 0.0 copy-done.5
  179.9 0.4 convolution_bitcast_fusion.1
  180.3 1.0 copy.12
  181.3 0.0 reduce-scatter.7.cloned.1.call-update
  182.0 2.0 gather_fusion.1
  184.0 0.9 select_select_fusion
  184.9 60.7 %reduce-scatter.7.cloned.1.call-done = f32[64,256]{1,0:T(8,128)} async-done(((f32[512,256]{1,0:T(8,128)}), f32[64,256]{1,0:T(8,128)}) %reduce-scatter.7.cloned.1.call-update) | async-done | bytes 65552
  (15 shorter events, 0.2 us)
Async XLA Ops:
  7.2 1.0 copy-start
  7.2 38.2 %all-reduce.4.cloned.1.call-start = ((), (), s32[]{:S(2)}) async-start(), calls=%async_computation.2 | async-start | bytes 262144 | tf_op jit(solution)/shard_map/psum | solution.py:12
  9.9 0.7 copy-start.7
  9.9 0.9 copy-start.6
  9.9 135.8 %reduce-scatter.5.cloned.1.call-start = ((), (), s32[]{:S(2)}) async-start(), calls=%async_computation.3 | async-start | bytes 1179648 | tf_op jit(solution)/shard_map/reduce_scatter | solution.py:39
  45.4 1.1 copy-start.2
  46.7 31.5 %copy-start.1 = (bf16[512,256]{1,0:T(8,128)(2,1)S(1)}, bf16[512,256]{1,0:T(8,128)(2,1)}, u32[]{:S(2)}) copy-start(bf16[512,256]{1,0:T(8,128)(2,1)} %param.10) | copy-start | bytes 786436
  79.8 1.0 copy-start.3
  80.8 97.9 %all-reduce.6.cloned.1.call-start = ((), (), s32[]{:S(2)}) async-start(), calls=%async_computation.4 | async-start | bytes 262144 | tf_op jit(solution)/shard_map/psum | solution.py:42
  80.9 0.7 copy-start.8
  145.7 99.9 %reduce-scatter.7.cloned.1.call-start = ((), (), s32[]{:S(2)}) async-start(), calls=%async_computation.5 | async-start | bytes 589824
  178.7 1.2 copy-start.4
  178.7 1.2 copy-start.5
Sparse Core Ops, SparseCore 0:
  10.9 34.4 all-reduce.3
  81.0 64.6 reduce-scatter.4
  148.0 30.6 all-reduce.5
  182.5 63.0 reduce-scatter.6
where the time goes:
time: 252 us
  waiting for transfers between devices  129 us (51%)
  blocking collectives  92.1 us (37%)
  between operations  15.2 us (6%)
  local copies, waits for them, and re-layouts  7.85 us (3%)
  other arithmetic  3.94 us (2%)
  matrix products  3.58 us (1%)
    unnamed x5, waiting for transfers between devices  60.7 us
    reduce_scatter x1, waiting for transfers between devices, local(): lax.psum_scatter(numer_all, 'blk', scatter_dimension=0, tiled=True)  35.3 us
    all_gather x1, blocking collectives, local(): all_fresh = lax.all_gather(fresh_keys, 'blk', axis=0, tiled=True)  33 us
    psum x1, waiting for transfers between devices, local(): numerator, denominator = lax.psum((numer_part, denom_part), 'group')  32.4 us
    all_gather x1, blocking collectives, local(): all_queries = lax.all_gather(query_rows, 'blk', axis=0, tiled=True)  31.5 us
    unnamed x1, blocking collectives  21.5 us
    psum x1, blocking collectives, local(): numerator, denominator = lax.psum((numer_part, denom_part), 'group')  6.03 us
  transfers between devices with their start and end apart: 4, of which 4 were waited for; matrix products, arithmetic and copies ran while one was open for 2% of the time, Pallas kernels for 0%

commit v1 on v0

--- a/solution.py
+++ b/solution.py
@@ -13,7 +13,12 @@
     length = jnp.sqrt(jnp.sum(projected * projected, axis=1, keepdims=True) + epsilon)
     unit_rows = projected / length
     query_rows = unit_rows.astype(jnp.bfloat16)
-    all_fresh = lax.all_gather(fresh_keys, "blk", axis=0, tiled=True)
+    ring = [fresh_keys]
+    for hop in range(7):
+        ring.append(lax.ppermute(ring[-1], "blk", [(dev, (dev + 1) % 8) for dev in range(8)]))
+    all_fresh = jnp.roll(
+        jnp.concatenate(ring[::-1], axis=0), (lax.axis_index("blk") + 1) * ring[0].shape[0], axis=0
+    )
     all_queries = lax.all_gather(query_rows, "blk", axis=0, tiled=True)
     query_total = all_queries.shape[0]
     key_width = all_queries.shape[1]

time: 252 us -> 264 us (1.048)
  waiting for transfers between devices: 129 us -> 172 us
  blocking collectives: 92.1 us -> 56.6 us
  starting transfers between devices: 0.16 us -> 4.71 us
    ppermute x0 -> x7, waiting for transfers between devices: none -> 37.3 us  [local(): lax.ppermute(ring[-1], 'blk', [(dev, (dev + 1) % 8) for dev in range(8)])]
    all_gather x1 -> x0, blocking collectives: 33 us -> none  [local(): all_fresh = lax.all_gather(fresh_keys, 'blk', axis=0, tiled=True)]
    psum x1, waiting for transfers between devices: 0.8 us -> 7.16 us  [local(): projected = lax.psum(partial_proj, 'group')]
    ppermute x0 -> x7, starting transfers between devices: none -> 4.55 us  [local(): lax.ppermute(ring[-1], 'blk', [(dev, (dev + 1) % 8) for dev in range(8)])]
  transfers between devices with their start and end apart: 4 -> 11, of which waited for: 4 -> 10; matrix products, arithmetic and copies ran while one was open for 2% -> 3% of each run, Pallas kernels for 0% -> 0%
where the time goes in v1:
time: 264 us; the launch traced here: 263 us
  waiting for transfers between devices  172 us (65%)
  blocking collectives  56.6 us (21%)
  between operations  15.4 us (6%)
  local copies, waits for them, and re-layouts  7.2 us (3%)
  starting transfers between devices  4.71 us (2%)
  other arithmetic  3.87 us (1%)
  matrix products  3.57 us (1%)
    unnamed x5, waiting for transfers between devices  60.3 us
    ppermute x7, waiting for transfers between devices, local(): lax.ppermute(ring[-1], 'blk', [(dev, (dev + 1) % 8) for dev in range(8)])  37.3 us
    reduce_scatter x1, waiting for transfers between devices, local(): lax.psum_scatter(numer_all, 'blk', scatter_dimension=0, tiled=True)  34.7 us
    psum x1, waiting for transfers between devices, local(): numerator, denominator = lax.psum((numer_part, denom_part), 'group')  32.5 us
    all_gather x1, blocking collectives, local(): all_queries = lax.all_gather(query_rows, 'blk', axis=0, tiled=True)  31.4 us
    unnamed x1, blocking collectives  19.2 us
    psum x1, waiting for transfers between devices, local(): projected = lax.psum(partial_proj, 'group')  7.16 us
    psum x1, blocking collectives, local(): numerator, denominator = lax.psum((numer_part, denom_part), 'group')  6.06 us
  transfers between devices with their start and end apart: 11, of which 10 were waited for; matrix products, arithmetic and copies ran while one was open for 3% of the time, Pallas kernels for 0%

profile of v1, /device:TPU:0, one launch (start us, length us, event | category | flops | bytes accessed | tf_op | source)
XLA Modules:
  0.0 263.3 jit_solution(697753017806172590)
XLA Ops:
  7.2 0.0 copy-start
  7.2 0.0 all-reduce.4.cloned.1.call-start
  7.2 3.0 %collective-permute-start = (bf16[128,256]{1,0:T(8,128)(2,1)}, bf16[128,256]{1,0:T(8,128)(2,1)S(1)}, u32[]{:S(2)}, u32[]{:S(2)}) collective-permute-start(bf16[128,256]{1,0:T(8,128)(2,1)} %param.11), channel_id=1, source_target_pairs={{0,1},{1,2},{2,3},{3,4},{4,5},{5,6},{6,7},{7,0},{8,9},{9,10},{10,1... | collective-permute-start | bytes 196616 | tf_op jit(solution)/shard_map/ppermute | solution.py:18
  10.2 5.5 %collective-permute-done = bf16[128,256]{1,0:T(8,128)(2,1)S(1)} collective-permute-done((bf16[128,256]{1,0:T(8,128)(2,1)}, bf16[128,256]{1,0:T(8,128)(2,1)S(1)}, u32[]{:S(2)}, u32[]{:S(2)}) %collective-permute-start) | collective-permute-done | bytes 65568 | tf_op jit(solution)/shard_map/ppermute | solution.py:18
  15.7 1.7 fusion.20
  17.5 0.0 all-reduce.4.cloned.1.call-update
  17.5 0.0 reduce-scatter.5.cloned.1.call-start
  17.6 5.1 %collective-permute-done.1 = bf16[128,256]{1,0:T(8,128)(2,1)S(1)} collective-permute-done((bf16[128,256]{1,0:T(8,128)(2,1)S(1)}, bf16[128,256]{1,0:T(8,128)(2,1)S(1)}, u32[]{:S(2)}, u32[]{:S(2)}) %collective-permute-start.1) | collective-permute-done | bytes 65568 | tf_op jit(solution)/shard_map/ppermute | solution.py:18
  22.7 6.9 %collective-permute-done.2 = bf16[128,256]{1,0:T(8,128)(2,1)S(1)} collective-permute-done((bf16[128,256]{1,0:T(8,128)(2,1)S(1)}, bf16[128,256]{1,0:T(8,128)(2,1)S(1)}, u32[]{:S(2)}, u32[]{:S(2)}) %collective-permute-start.2) | collective-permute-done | bytes 65568 | tf_op jit(solution)/shard_map/ppermute | solution.py:18
  29.7 6.9 %collective-permute-done.3 = bf16[128,256]{1,0:T(8,128)(2,1)S(1)} collective-permute-done((bf16[128,256]{1,0:T(8,128)(2,1)S(1)}, bf16[128,256]{1,0:T(8,128)(2,1)S(1)}, u32[]{:S(2)}, u32[]{:S(2)}) %collective-permute-start.3) | collective-permute-done | bytes 65568 | tf_op jit(solution)/shard_map/ppermute | solution.py:18
  36.6 7.3 %collective-permute-done.4 = bf16[128,256]{1,0:T(8,128)(2,1)S(1)} collective-permute-done((bf16[128,256]{1,0:T(8,128)(2,1)S(1)}, bf16[128,256]{1,0:T(8,128)(2,1)S(1)}, u32[]{:S(2)}, u32[]{:S(2)}) %collective-permute-start.4) | collective-permute-done | bytes 65568 | tf_op jit(solution)/shard_map/ppermute | solution.py:18
  43.9 7.2 %all-reduce.4.cloned.1.call-done = f32[128,256]{1,0:T(8,128)} async-done(((f32[128,256]{1,0:T(8,128)}), f32[128,256]{1,0:T(8,128)}) %all-reduce.4.cloned.1.call-update) | async-done | bytes 131088 | tf_op jit(solution)/shard_map/psum | solution.py:12
  51.1 1.0 multiply_reduce_fusion.1
  52.1 1.5 collective-permute-start.6
  53.6 5.5 %collective-permute-done.6 = bf16[128,256]{1,0:T(8,128)(2,1)S(1)} collective-permute-done((bf16[128,256]{1,0:T(8,128)(2,1)S(1)}, bf16[128,256]{1,0:T(8,128)(2,1)S(1)}, u32[]{:S(2)}, u32[]{:S(2)}) %collective-permute-start.6) | collective-permute-done | bytes 65568 | tf_op jit(solution)/shard_map/ppermute | solution.py:18
  59.2 0.0 copy-start.4
  59.2 0.8 copy-done.4
  60.2 0.8 gather_fusion
  61.1 0.0 copy-done.2
  61.1 0.2 fusion.6
  61.3 0.0 copy-start.1
  61.3 31.4 %all_gather.3 = bf16[1024,256]{1,0:T(8,128)(2,1)S(1)} all-gather(bf16[128,256]{1,0:T(8,128)(2,1)S(1)} %get-tuple-element.53), channel_id=1, replica_groups=mesh['group'=4,'blk'=8] {'blk'}, dimensions={0}, use_global_device_ids=true | all-gather | bytes 589824 | tf_op jit(solution)/shard_map/all_gather | solution.py:22
  92.7 1.6 while.12
  92.7 0.4 fusion.35
  93.1 0.3 fusion.36
  93.5 0.4 fusion.35
  93.9 0.3 fusion.36
  94.3 1.0 copy-done.3
  95.3 0.0 reduce-scatter.5.cloned.1.call-update
  95.3 0.0 all-reduce.6.cloned.1.call-start
  95.3 0.0 copy-start.8
  95.4 0.6 copy-done.8
  96.0 0.6 dynamic-slice
  97.3 19.2 %all-reduce = f32[1024]{0:T(1024)S(1)} all-reduce(f32[1024]{0:T(1024)S(1)} %bitcast.43), channel_id=2, replica_groups=mesh['group'=4,'blk'=8] {'blk'}, use_global_device_ids=true, to_apply=%region_6.7.clone | all-reduce | flops 1024 | bytes 8192
  116.4 0.1 dynamic-slice.1
  116.5 6.1 %psum.22 = f32[128]{0:T(128)S(1)} all-reduce(f32[128]{0:T(128)S(1)} %dynamic-slice.1), channel_id=1, replica_groups=mesh['group'=4,'blk'=8] {'group'}, use_global_device_ids=true, to_apply=%region_7.8 | all-reduce | flops 128 | bytes 1024 | tf_op jit(solution)/shard_map/psum | solution.py:47
  122.6 34.7 %reduce-scatter.5.cloned.1.call-done = f32[128,256]{1,0:T(8,128)} async-done(((f32[1024,256]{1,0:T(8,128)}), f32[128,256]{1,0:T(8,128)}) %reduce-scatter.5.cloned.1.call-update) | async-done | bytes 131088 | tf_op jit(solution)/shard_map/reduce_scatter | solution.py:44
  157.3 0.0 all-reduce.6.cloned.1.call-update
  157.3 0.0 reduce-scatter.7.cloned.1.call-start
  157.4 0.5 fusion.15
  157.9 32.5 %all-reduce.6.cloned.1.call-done = f32[128,256]{1,0:T(8,128)} async-done(((f32[128,256]{1,0:T(8,128)}), f32[128,256]{1,0:T(8,128)}) %all-reduce.6.cloned.1.call-update) | async-done | bytes 131088 | tf_op jit(solution)/shard_map/psum | solution.py:47
  190.4 1.2 multiply_reduce_fusion
  191.6 0.4 convolution_bitcast_fusion.1
  191.9 1.0 copy.12
  192.9 0.0 reduce-scatter.7.cloned.1.call-update
  193.7 2.0 gather_fusion.1
  195.6 0.9 select_select_fusion
  196.5 60.2 %reduce-scatter.7.cloned.1.call-done = f32[64,256]{1,0:T(8,128)} async-done(((f32[512,256]{1,0:T(8,128)}), f32[64,256]{1,0:T(8,128)}) %reduce-scatter.7.cloned.1.call-update) | async-done | bytes 65552
  (45 shorter events, 0.3 us)
Async XLA Ops:
  7.2 8.6 %copy-start = (bf16[512,256]{1,0:T(8,128)(2,1)S(1)}, bf16[512,256]{1,0:T(8,128)(2,1)}, u32[]{:S(2)}) copy-start(bf16[512,256]{1,0:T(8,128)(2,1)} %param.9) | copy-start | bytes 786436
  7.2 43.9 %all-reduce.4.cloned.1.call-start = ((), (), s32[]{:S(2)}) async-start(), calls=%async_computation.2 | async-start | bytes 262144 | tf_op jit(solution)/shard_map/psum | solution.py:12
  7.2 8.5 %collective-permute-start = (bf16[128,256]{1,0:T(8,128)(2,1)}, bf16[128,256]{1,0:T(8,128)(2,1)S(1)}, u32[]{:S(2)}, u32[]{:S(2)}) collective-permute-start(bf16[128,256]{1,0:T(8,128)(2,1)} %param.11), channel_id=1, source_target_pairs={{0,1},{1,2},{2,3},{3,4},{4,5},{5,6},{6,7},{7,0},{8,9},{9,10},{10,1... | collective-permute-start | bytes 196616 | tf_op jit(solution)/shard_map/ppermute | solution.py:18
  15.7 7.0 %collective-permute-start.1 = (bf16[128,256]{1,0:T(8,128)(2,1)S(1)}, bf16[128,256]{1,0:T(8,128)(2,1)S(1)}, u32[]{:S(2)}, u32[]{:S(2)}) collective-permute-start(bf16[128,256]{1,0:T(8,128)(2,1)S(1)} %collective-permute-done), channel_id=1, source_target_pairs={{0,1},{1,2},{2,3},{3,4},{4,5},{5,6},{6,7},{7,0},{8,9},{9,10},{10,1... | collective-permute-start | bytes 196616 | tf_op jit(solution)/shard_map/ppermute | solution.py:18
  17.5 5.2 %copy-start.7 = (s32[128]{0:T(128)S(1)}, s32[128]{0:T(128)}, u32[]{:S(2)}) copy-start(s32[128]{0:T(128)} %param.12) | copy-start | bytes 1540
  17.5 139.8 %reduce-scatter.5.cloned.1.call-start = ((), (), s32[]{:S(2)}) async-start(), calls=%async_computation.3 | async-start | bytes 1179648 | tf_op jit(solution)/shard_map/reduce_scatter | solution.py:44
  22.7 7.0 %collective-permute-start.2 = (bf16[128,256]{1,0:T(8,128)(2,1)S(1)}, bf16[128,256]{1,0:T(8,128)(2,1)S(1)}, u32[]{:S(2)}, u32[]{:S(2)}) collective-permute-start(bf16[128,256]{1,0:T(8,128)(2,1)S(1)} %collective-permute-done.1), channel_id=1, source_target_pairs={{0,1},{1,2},{2,3},{3,4},{4,5},{5,6},{6,7},{7,0},{8,9},{9,10},{10,1... | collective-permute-start | bytes 196616 | tf_op jit(solution)/shard_map/ppermute | solution.py:18
  29.7 7.0 %collective-permute-start.3 = (bf16[128,256]{1,0:T(8,128)(2,1)S(1)}, bf16[128,256]{1,0:T(8,128)(2,1)S(1)}, u32[]{:S(2)}, u32[]{:S(2)}) collective-permute-start(bf16[128,256]{1,0:T(8,128)(2,1)S(1)} %collective-permute-done.2), channel_id=1, source_target_pairs={{0,1},{1,2},{2,3},{3,4},{4,5},{5,6},{6,7},{7,0},{8,9},{9,10},{10,1... | collective-permute-start | bytes 196616 | tf_op jit(solution)/shard_map/ppermute | solution.py:18
  36.6 7.3 %collective-permute-start.4 = (bf16[128,256]{1,0:T(8,128)(2,1)S(1)}, bf16[128,256]{1,0:T(8,128)(2,1)S(1)}, u32[]{:S(2)}, u32[]{:S(2)}) collective-permute-start(bf16[128,256]{1,0:T(8,128)(2,1)S(1)} %collective-permute-done.3), channel_id=1, source_target_pairs={{0,1},{1,2},{2,3},{3,4},{4,5},{5,6},{6,7},{7,0},{8,9},{9,10},{10,1... | collective-permute-start | bytes 196616 | tf_op jit(solution)/shard_map/ppermute | solution.py:18
  43.9 8.2 %collective-permute-start.5 = (bf16[128,256]{1,0:T(8,128)(2,1)S(1)}, bf16[128,256]{1,0:T(8,128)(2,1)S(1)}, u32[]{:S(2)}, u32[]{:S(2)}) collective-permute-start(bf16[128,256]{1,0:T(8,128)(2,1)S(1)} %collective-permute-done.4), channel_id=1, source_target_pairs={{0,1},{1,2},{2,3},{3,4},{4,5},{5,6},{6,7},{7,0},{8,9},{9,10},{10,1... | collective-permute-start | bytes 196616 | tf_op jit(solution)/shard_map/ppermute | solution.py:18
  52.1 7.0 %collective-permute-start.6 = (bf16[128,256]{1,0:T(8,128)(2,1)S(1)}, bf16[128,256]{1,0:T(8,128)(2,1)S(1)}, u32[]{:S(2)}, u32[]{:S(2)}) collective-permute-start(bf16[128,256]{1,0:T(8,128)(2,1)S(1)} %collective-permute-done.5), channel_id=1, source_target_pairs={{0,1},{1,2},{2,3},{3,4},{4,5},{5,6},{6,7},{7,0},{8,9},{9,10},{10,1... | collective-permute-start | bytes 196616 | tf_op jit(solution)/shard_map/ppermute | solution.py:18
  59.2 0.8 copy-start.4
  60.2 0.9 copy-start.2
  61.3 31.4 %copy-start.1 = (bf16[512,256]{1,0:T(8,128)(2,1)S(1)}, bf16[512,256]{1,0:T(8,128)(2,1)}, u32[]{:S(2)}) copy-start(bf16[512,256]{1,0:T(8,128)(2,1)} %param.10) | copy-start | bytes 786436
  94.3 1.0 copy-start.3
  95.3 95.1 %all-reduce.6.cloned.1.call-start = ((), (), s32[]{:S(2)}) async-start(), calls=%async_computation.4 | async-start | bytes 262144 | tf_op jit(solution)/shard_map/psum | solution.py:47
  95.3 0.7 copy-start.8
  157.3 99.5 %reduce-scatter.7.cloned.1.call-start = ((), (), s32[]{:S(2)}) async-start(), calls=%async_computation.5 | async-start | bytes 589824
  190.3 1.2 copy-start.5
  190.3 1.2 copy-start.6
Sparse Core Ops, SparseCore 0:
  17.6 33.4 all-reduce.3
  95.4 61.8 reduce-scatter.4
  159.6 30.6 all-reduce.5
  194.1 62.6 reduce-scatter.6
